TPU v7x, 32 devices: a whole 2x2x4 slice. The times are simulated.
32 devices in a mesh: view: 4 (over z), tile: 8 (over y, x, core).
Axes of the slice: x: 2, y: 2, z: 4, core: 2. Of those that a mesh axis runs over, the one named last changes fastest.
Arguments:
- sdf_value: float32 [6144, 256], P(('view', 'tile')), may hold values from -1 to 1
- weight: float32 [6144, 256], P(('view', 'tile')), may hold values from 0.25 to 4
- color: float32 [3, 6144, 256], P(None, ('view', 'tile')), may hold values from 0 to 1
- voxel_index: int32 [6144, 256], P(('view', 'tile')), may hold values from 0 to 511
- valid: int32 [6144, 256], P(('view', 'tile')), may hold values 0 or 1
- list_count: int32 [6144], P(('view', 'tile')), may hold values from 1 to 256
- list_key: int32 [6144], P(('view', 'tile')), may hold values from 0 to 2047, as said below
- owner_slot: int32 [2048], replicated, may hold values from 0 to 2047, as said below
Outputs:
- joined_tsdf: float32 [2048, 512], P(('view', 'tile'))
- joined_color: float32 [2048, 3, 512], P(('view', 'tile'))
- block_counts: int32 [2048], replicated
Inputs may be any that keep to these rules, and one draw needn't show every extreme that they name: `owner_slot`: each block key has one storage row and each row one key. Of the 192 lists of one device, at most 24 have a storage row owner_slot[list_key] among the 64 rows of any one device; some device receives exactly 24 lists from every device.
All inputs are finite; a program needn't handle non-finite values. No bound on the sum of `valid` on one device may be relied on, other than what follows from the above.
Results may differ from a plain program's by a relative error of at most 0.0037.
Values may be sent and summed in bfloat16 or wider, within the bound.
A program may use at most 64 MiB of HBM per device.

v0:
```python
import jax
import jax.numpy as jnp
from jax import lax
from jax.sharding import PartitionSpec as P

VOX = 512


def deliver(parcels):
    return (
        lax.all_to_all(
            parcels[0].astype(jnp.bfloat16),
            ("view", "tile"),
            split_axis=0,
            concat_axis=0,
            tiled=True,
        ).astype(jnp.float32),
        lax.all_to_all(parcels[1], ("view", "tile"), split_axis=0, concat_axis=0, tiled=True),
    )


def on_device(sdf_value, weight, color, voxel_index, valid, list_count, list_key, owner_slot):
    list_rows, points = sdf_value.shape
    devices = lax.axis_size(("view", "tile"))
    blocks_all = owner_slot.shape[0]
    blocks_dev = blocks_all // devices
    block_capacity = 4 * list_rows // devices
    total_slots = devices * block_capacity
    position = jnp.arange(points, dtype=jnp.int32)
    live_mask = ((position[None, :] < list_count[:, None]) & (valid == 1)).astype(jnp.float32)
    scaled = live_mask * weight
    payload = jnp.stack(
        [
            live_mask,
            scaled,
            scaled * sdf_value,
            scaled * color[0],
            scaled * color[1],
            scaled * color[2],
        ],
        axis=1,
    ).astype(jnp.bfloat16)
    key_match = list_key[:, None] == jnp.arange(blocks_all, dtype=jnp.int32)[None, :]
    storage = jnp.sum(jnp.where(key_match, owner_slot[None, :], 0), axis=1)
    owner_dev = storage // blocks_dev
    block_row = storage % blocks_dev
    owner_hot = (owner_dev[:, None] == jnp.arange(devices, dtype=jnp.int32)[None, :]).astype(
        jnp.int32
    )
    arrival_order = jnp.sum(jnp.cumsum(owner_hot, axis=0) * owner_hot, axis=1) - 1
    slot_index = owner_dev * block_capacity + arrival_order
    placement = slot_index[None, :] == jnp.arange(total_slots, dtype=jnp.int32)[:, None]
    send_rows = jnp.full((total_slots,), -1, jnp.int32).at[slot_index].set(block_row)
    block_ids = jnp.arange(blocks_dev, dtype=jnp.int32)
    voxel_ids = jnp.arange(VOX, dtype=jnp.int32)
    voxel_onehot = (voxel_index[:, :, None] == voxel_ids[None, None, :]).astype(jnp.bfloat16)
    partial_value = jnp.einsum(
        "lcp,lpv->lcv", payload, voxel_onehot, preferred_element_type=jnp.float32
    )
    send_parts = jnp.dot(
        placement.astype(jnp.float32),
        partial_value.reshape(list_rows, -1),
        precision=lax.Precision.HIGHEST,
        preferred_element_type=jnp.float32,
    )
    got_parts, got_rows = deliver((send_parts, send_rows))
    row_hot = (got_rows[:, None] == block_ids[None, :]).astype(jnp.float32)
    voxel_sums = jnp.einsum(
        "gb,gk->bk",
        row_hot,
        got_parts,
        precision=lax.Precision.HIGHEST,
        preferred_element_type=jnp.float32,
    )
    voxel_sums = voxel_sums.reshape(blocks_dev, 6, VOX)
    local_counts = jnp.sum(voxel_sums[:, 0, :], axis=1).astype(jnp.int32)
    block_counts = lax.all_gather(local_counts, ("view", "tile"), axis=0, tiled=True)
    divisor = jnp.maximum(voxel_sums[:, 1, :], 1.0)
    joined_tsdf = voxel_sums[:, 2, :] / divisor
    joined_color = voxel_sums[:, 3:6, :] / divisor[:, None, :]
    return (joined_tsdf, joined_color, block_counts)


def solution(mesh):
    return jax.shard_map(
        on_device,
        mesh=mesh,
        in_specs=(
            P(("view", "tile"), None),
            P(("view", "tile"), None),
            P(None, ("view", "tile"), None),
            P(("view", "tile"), None),
            P(("view", "tile"), None),
            P(("view", "tile")),
            P(("view", "tile")),
            P(),
        ),
        out_specs=(P(("view", "tile"), None), P(("view", "tile"), None, None), P()),
        check_vma=False,
    )
```

profile of v0, /device:TPU:1, one launch (start us, length us, event | category | flops | bytes accessed | tf_op | source)
XLA Modules:
  0.0 210.0 jit_solution(8750741715965171564)
XLA Ops:
  0.6 0.0 copy-start
  0.6 1.1 select_reduce_fusion
  1.8 0.6 reduce-window.6
  2.4 0.2 slice_reduce_fusion.1
  2.6 0.1 bitcast_bitcast_fusion
  2.7 1.2 scatter_custom_fusion
  4.0 0.7 all_to_all.14
  4.6 7.1 %all-to-all-start = ((s32[32,24,1]{1,2,0:T(1,128)}), s32[32,24,1]{1,2,0:T(1,128)S(1)}, u32[]{:S(2)}, u32[]{:S(2)}) async-start(s32[32,24,1]{1,2,0:T(1,128)} %bitcast.4), calls=%async_computation | async-start | bytes 32768 | tf_op jit(solution)/shard_map/all_to_all | solution.py:18
  11.7 1.2 fusion.16
  13.0 1.0 convert_bitcast_fusion
  14.0 1.3 fusion.15
  15.3 0.2 copy.81
  15.4 0.2 copy.82
  15.6 0.2 copy.83
  15.7 0.2 copy.79
  15.9 0.2 copy.80
  16.1 0.2 copy.84
  16.2 1.8 stack.37
  18.0 0.0 copy-done
  18.1 23.8 %fusion = f32[192,6,512]{2,1,0:T(8,128)S(1)} fusion(bf16[192,6,256]{2,1,0:T(8,128)(2,1)S(1)} %stack.37, s32[192,256]{1,0:T(8,128)S(1)} %copy-done), kind=kOutput, calls=%fused_computation.2 | convolution fusion | flops 327155712 | bytes 3145728 | tf_op jit(solution)/shard_map/lcp,lpv->lcv/dot_general | solution.py:57
  41.8 2.0 copy.88
  43.9 5.7 %convolution_convert_fusion = bf16[768,3072]{1,0:T(8,128)(2,1)} fusion(f32[192,3072]{1,0:T(8,128)S(1)} %bitcast.67, s32[192]{0:T(256)S(1)} %get-tuple-element.14), kind=kOutput, calls=%fused_computation.4 | convolution fusion | flops 5438324736 | bytes 7078656 | tf_op jit(solution)/shard_map/dot_general | solution.py:60
  49.6 0.0 all-to-all-done
  49.6 5.9 %all-to-all-start.1 = ((bf16[32,24,3072]{2,1,0:T(8,128)(2,1)}), bf16[32,24,3072]{2,1,0:T(8,128)(2,1)}, u32[]{:S(2)}, u32[]{:S(2)}) async-start(bf16[32,24,3072]{2,1,0:T(8,128)(2,1)} %bitcast.65), calls=%async_computation.1 | async-start | bytes 9437184 | tf_op jit(solution)/shard_map/all_to_all | solution.py:11
  55.5 0.5 broadcast.216
  56.0 0.7 reduce.6
  56.7 0.1 eq.91
  56.8 103.1 %all-to-all-done.1 = bf16[32,24,3072]{2,1,0:T(8,128)(2,1)} async-done(((bf16[32,24,3072]{2,1,0:T(8,128)(2,1)}), bf16[32,24,3072]{2,1,0:T(8,128)(2,1)}, u32[]{:S(2)}, u32[]{:S(2)}) %all-to-all-start.1) | async-done | bytes 4718624 | tf_op jit(solution)/shard_map/all_to_all | solution.py:11
  159.9 6.7 %copy.85 = bf16[768,3072]{0,1:T(8,128)(2,1)} copy(bf16[768,3072]{1,0:T(8,128)(2,1)} %bitcast.16) | data formatting | bytes 9437184 | tf_op jit(solution)/shard_map/all_to_all | solution.py:11
  166.6 3.9 %fusion.7 = f32[64,6,512]{2,0,1:T(8,128)S(1)} fusion(bf16[6,512,768]{2,1,0:T(8,128)(2,1)} %bitcast.66, s32[768]{0:T(1024)S(1)} %eq.91), kind=kOutput, calls=%fused_computation.21 | convolution fusion | flops 302039040 | bytes 5508096 | tf_op jit(solution)/shard_map/gb,gk->bk/dot_general | solution.py:68
  170.5 0.8 slice_reduce_fusion
  171.3 0.8 slice_divide_fusion
  172.1 0.1 convert_dynamic-update-slice_fusion
  172.2 37.8 %all-reduce.1 = s32[2048]{0:T(1024)} all-reduce(s32[2048]{0:T(1024)S(1)} %convert_dynamic-update-slice_fusion), channel_id=1, replica_groups=mesh['view'=4,'tile'=8] {'view','tile'}, use_global_device_ids=true, to_apply=%add.1 | all-reduce | flops 2048 | bytes 16384
  (10 shorter events, 0.1 us)
Async XLA Ops:
  0.6 17.4 %copy-start = (s32[192,256]{1,0:T(8,128)S(1)}, s32[192,256]{1,0:T(8,128)}, u32[]{:S(2)}) copy-start(s32[192,256]{1,0:T(8,128)} %param.11) | copy-start | bytes 589828
  4.6 45.0 %all-to-all-start = ((s32[32,24,1]{1,2,0:T(1,128)}), s32[32,24,1]{1,2,0:T(1,128)S(1)}, u32[]{:S(2)}, u32[]{:S(2)}) async-start(s32[32,24,1]{1,2,0:T(1,128)} %bitcast.4), calls=%async_computation | async-start | bytes 32768 | tf_op jit(solution)/shard_map/all_to_all | solution.py:18
  49.6 110.3 %all-to-all-start.1 = ((bf16[32,24,3072]{2,1,0:T(8,128)(2,1)}), bf16[32,24,3072]{2,1,0:T(8,128)(2,1)}, u32[]{:S(2)}, u32[]{:S(2)}) async-start(bf16[32,24,3072]{2,1,0:T(8,128)(2,1)} %bitcast.65), calls=%async_computation.1 | async-start | bytes 9437184 | tf_op jit(solution)/shard_map/all_to_all | solution.py:11
where the time goes:
time: 212 us; the launch traced here: 210 us
  waiting for transfers between devices  103 us (49%)
  blocking collectives  37.8 us (18%)
  matrix products  33.4 us (16%)
  local copies, waits for them, and re-layouts  14.2 us (7%)
  starting transfers between devices  13 us (6%)
  other arithmetic  7.74 us (4%)
    all_to_all x1, waiting for transfers between devices, deliver(): lax.all_to_all(parcels[0].astype(jnp.bfloat16), ('view', 'tile'), split_a...  103 us
    unnamed x1, blocking collectives  37.8 us
    dot_general x1, matrix products, on_device(): jnp.einsum('lcp,lpv->lcv', payload, voxel_onehot, preferred_element_type=...  23.8 us
    all_to_all x1, starting transfers between devices, deliver(): lax.all_to_all(parcels[1], ('view', 'tile'), split_axis=0, concat_axis=0,...  7.08 us
    all_to_all x1, local copies, waits for them, and re-layouts, deliver(): lax.all_to_all(parcels[0].astype(jnp.bfloat16), ('view', 'tile'), split_a...  6.71 us
    all_to_all x1, starting transfers between devices, deliver(): lax.all_to_all(parcels[0].astype(jnp.bfloat16), ('view', 'tile'), split_a...  5.88 us
    dot_general x1, matrix products, on_device(): jnp.dot(placement.astype(jnp.float32), partial_value.reshape(list_rows, -...  5.72 us
  transfers between devices with their start and end apart: 2, of which 1 were waited for; matrix products, arithmetic and copies ran while one was open for 19% of the time, Pallas kernels for 0%

commit v1 on v0

v1 whole, which is shorter than its diff:
```python
import functools

import jax
import jax.numpy as jnp
from jax import lax
from jax.experimental import pallas as pl
from jax.experimental.pallas import tpu as pltpu
from jax.sharding import PartitionSpec as P

VOX = 512
HI = 8
LO = VOX // HI
CH = 5
AXES = ("view", "tile")
NT = (((1,), (1,)), ((), ()))


def pack_kernel(n, cap, slot_ref, live_count_ref, sdf_ref, weight_ref, color_ref, voxel_ref, valid_ref, out_ref):
    lists, points = sdf_ref.shape
    position = lax.broadcasted_iota(jnp.int32, (lists, points), 1)
    live = (position < live_count_ref[...]) & (valid_ref[...] == 1)
    scaled = jnp.where(live, weight_ref[...], 0.0)
    slots = lax.broadcasted_iota(jnp.int32, (n * cap, lists), 0)
    placement = jnp.where(slots == slot_ref[...], 1.0, 0.0).astype(jnp.bfloat16)
    for c in range(CH + 1):
        if c == 0:
            value = scaled
        elif c == 1:
            value = scaled * sdf_ref[...]
        elif c < CH:
            value = scaled * color_ref[c - 2]
        else:
            value = (voxel_ref[...] - VOX // 2).astype(jnp.float32)
        placed = jnp.dot(
            placement, value.astype(jnp.bfloat16), preferred_element_type=jnp.float32
        ).astype(jnp.bfloat16)
        for d in range(n):
            out_ref[d, c * cap : (c + 1) * cap, :] = placed[d * cap : (d + 1) * cap, :]


def join_kernel(
    n, tiles, cap, group, q, send_ref, meta_ref, tsdf_ref, color_ref, counts_ref,
    got, got_meta, block, parts, acc, hist, send_sem, recv_sem, meta_send_sem, meta_recv_sem,
):
    me = lax.axis_index("view") * tiles + lax.axis_index("tile")
    points = send_ref.shape[-1]
    blocks_dev = tsdf_ref.shape[0]
    rows = CH * HI

    def mesh_id(d):
        return (d // tiles, d % tiles)

    barrier = pltpu.get_barrier_semaphore()

    @pl.loop(1, n)
    def _(i):
        pl.semaphore_signal(
            barrier, inc=1, device_id=mesh_id(lax.rem(me + i, n)),
            device_id_type=pl.DeviceIdType.MESH,
        )

    own = pltpu.make_async_copy(send_ref.at[me], got.at[0], recv_sem.at[0])
    own_meta = pltpu.make_async_copy(meta_ref.at[me], got_meta.at[0], meta_recv_sem.at[0])
    own.start()
    own_meta.start()
    acc[...] = jnp.zeros_like(acc)
    hist[...] = jnp.zeros_like(hist)
    pl.semaphore_wait(barrier, n - 1)

    def copies(i):
        d = lax.rem(me + i, n)
        return (
            pltpu.make_async_remote_copy(
                src_ref=meta_ref.at[d], dst_ref=got_meta.at[i],
                send_sem=meta_send_sem.at[i], recv_sem=meta_recv_sem.at[i],
                device_id=mesh_id(d), device_id_type=pl.DeviceIdType.MESH,
            ),
            pltpu.make_async_remote_copy(
                src_ref=send_ref.at[d], dst_ref=got.at[i],
                send_sem=send_sem.at[i], recv_sem=recv_sem.at[i],
                device_id=mesh_id(d), device_id_type=pl.DeviceIdType.MESH,
            ),
        )

    @pl.loop(1, n)
    def _(i):
        for copy in copies(i):
            copy.start()

    hi_ids = lax.broadcasted_iota(jnp.int32, (HI, points), 0).astype(jnp.float32)
    lo_ids = lax.broadcasted_iota(jnp.int32, (LO, points), 0).astype(jnp.float32)
    lanes = q * 128
    hist_hi = lax.broadcasted_iota(jnp.int32, (hist.shape[0], lanes), 0).astype(jnp.float32)
    hist_lo = lax.broadcasted_iota(jnp.int32, (128, lanes), 0).astype(jnp.float32)
    row_ids = lax.broadcasted_iota(jnp.int32, (blocks_dev, group * cap), 0).astype(jnp.float32)

    def one_source(i, j):
        pltpu.make_async_copy(got_meta.at[i], got_meta.at[i], meta_recv_sem.at[i]).wait()
        pltpu.make_async_copy(got.at[i], got.at[i], recv_sem.at[i]).wait()
        block[...] = got[i].astype(jnp.float32)
        voxel = block[CH * cap : (CH + 1) * cap, :] + float(VOX // 2)
        high = jnp.floor(voxel * (1.0 / LO))
        low = voxel - high * float(LO)
        for s in range(cap):
            mask = jnp.broadcast_to(high[s : s + 1, :], (HI, points)) == hi_ids
            a = jnp.concatenate(
                [
                    jnp.where(
                        mask,
                        jnp.broadcast_to(block[c * cap + s : c * cap + s + 1, :], (HI, points)),
                        0.0,
                    )
                    for c in range(CH)
                ],
                axis=0,
            ).astype(jnp.bfloat16)
            b = jnp.where(
                jnp.broadcast_to(low[s : s + 1, :], (LO, points)) == lo_ids, 1.0, 0.0
            ).astype(jnp.bfloat16)
            parts[j * cap + s] = lax.dot_general(a, b, NT, preferred_element_type=jnp.float32)
        meta = got_meta[i]
        storage = jnp.concatenate([meta[1 + k : 2 + k, :] for k in range(q)], axis=1)
        counts = jnp.concatenate([meta[1 + q + k : 2 + q + k, :] for k in range(q)], axis=1)
        s_hi = jnp.floor(storage * (1.0 / 128))
        s_lo = storage - s_hi * 128.0
        a = jnp.where(s_hi == hist_hi, counts, 0.0).astype(jnp.bfloat16)
        b = jnp.where(s_lo == hist_lo, 1.0, 0.0).astype(jnp.bfloat16)
        hist[...] += lax.dot_general(a, b, NT, preferred_element_type=jnp.float32)

    @pl.loop(0, n // group)
    def _(g):
        @pl.loop(0, group)
        def _(j):
            one_source(g * group + j, j)

        row = jnp.concatenate(
            [got_meta[g * group + j][0:1, 0:cap] for j in range(group)], axis=1
        )
        hot = jnp.where(row == row_ids, 1.0, 0.0).astype(jnp.bfloat16)
        for r in range(rows):
            acc[r] += jnp.dot(
                hot, parts[:, r, :].astype(jnp.bfloat16), preferred_element_type=jnp.float32
            )

    for h in range(HI):
        divisor = jnp.maximum(acc[h], 1.0)
        tsdf_ref[:, h * LO : (h + 1) * LO] = acc[HI + h] / divisor
        for k in range(3):
            color_ref[k, :, h * LO : (h + 1) * LO] = acc[(2 + k) * HI + h] / divisor
    counts_ref[...] = hist[...].astype(jnp.int32)

    @pl.loop(1, n)
    def _(i):
        for copy in copies(i):
            copy.wait_send()


def on_device(tiles, sdf_value, weight, color, voxel_index, valid, list_count, list_key, owner_slot):
    lists, points = sdf_value.shape
    n = lax.axis_size(AXES)
    blocks_all = owner_slot.shape[0]
    blocks_dev = blocks_all // n
    cap = 4 * lists // n
    q = -(-lists // 128)
    group = 1
    while 2 * group * cap <= 256 and n % (2 * group) == 0:
        group *= 2

    position = jnp.arange(points, dtype=jnp.int32)
    live_points = jnp.sum(
        ((position[None, :] < list_count[:, None]) & (valid == 1)).astype(jnp.int32), axis=1
    )
    key_match = list_key[:, None] == jnp.arange(blocks_all, dtype=jnp.int32)[None, :]
    storage = jnp.sum(jnp.where(key_match, owner_slot[None, :], 0), axis=1)
    owner = storage // blocks_dev
    row = storage % blocks_dev
    ids = jnp.arange(lists, dtype=jnp.int32)
    arrival = jnp.sum(
        ((owner[:, None] == owner[None, :]) & (ids[None, :] < ids[:, None])).astype(jnp.int32), axis=1
    )
    slot = owner * cap + arrival
    slot_row = (
        jnp.max(
            jnp.where(
                slot[None, :] == jnp.arange(n * cap, dtype=jnp.int32)[:, None], row[None, :], -1
            ),
            axis=1,
        )
        .astype(jnp.float32)
        .reshape(n, 1, cap)
    )
    slot_row = jnp.pad(slot_row, ((0, 0), (0, 0), (0, 128 - cap)), constant_values=-1.0)

    def lane_rows(x):
        x = jnp.pad(x.astype(jnp.float32), (0, q * 128 - lists)).reshape(1, q, 128)
        return jnp.broadcast_to(x, (n, q, 128))

    meta_rows = -(-(1 + 2 * q) // 8) * 8
    meta = jnp.concatenate(
        [
            slot_row,
            lane_rows(storage),
            lane_rows(live_points),
            jnp.zeros((n, meta_rows - 1 - 2 * q, 128), jnp.float32),
        ],
        axis=1,
    )
    send = pl.pallas_call(
        functools.partial(pack_kernel, n, cap),
        out_shape=jax.ShapeDtypeStruct((n, (CH + 1) * cap, points), jnp.bfloat16),
        in_specs=[pl.BlockSpec(memory_space=pltpu.VMEM)] * 7,
        out_specs=pl.BlockSpec(memory_space=pltpu.VMEM),
    )(slot[None, :], list_count[:, None], sdf_value, weight, color, voxel_index, valid)

    rows = CH * HI
    tsdf, joined, counts = pl.pallas_call(
        functools.partial(join_kernel, n, tiles, cap, group, q),
        out_shape=(
            jax.ShapeDtypeStruct((blocks_dev, VOX), jnp.float32),
            jax.ShapeDtypeStruct((3, blocks_dev, VOX), jnp.float32),
            jax.ShapeDtypeStruct((blocks_all // 128, 128), jnp.int32),
        ),
        in_specs=[pl.BlockSpec(memory_space=pl.ANY)] * 2,
        out_specs=(pl.BlockSpec(memory_space=pltpu.VMEM),) * 3,
        scratch_shapes=[
            pltpu.VMEM((n, (CH + 1) * cap, points), jnp.bfloat16),
            pltpu.VMEM((n, meta_rows, 128), jnp.float32),
            pltpu.VMEM(((CH + 1) * cap, points), jnp.float32),
            pltpu.VMEM((group * cap, rows, LO), jnp.float32),
            pltpu.VMEM((rows, blocks_dev, LO), jnp.float32),
            pltpu.VMEM((blocks_all // 128, 128), jnp.float32),
            pltpu.SemaphoreType.DMA((n,)),
            pltpu.SemaphoreType.DMA((n,)),
            pltpu.SemaphoreType.DMA((n,)),
            pltpu.SemaphoreType.DMA((n,)),
        ],
        compiler_params=pltpu.CompilerParams(collective_id=0, has_side_effects=True),
    )(send, meta)
    return tsdf, jnp.swapaxes(joined, 0, 1), counts.reshape(blocks_all)


def solution(mesh):
    return jax.shard_map(
        functools.partial(on_device, mesh.shape["tile"]),
        mesh=mesh,
        in_specs=(
            P(AXES, None),
            P(AXES, None),
            P(None, AXES, None),
            P(AXES, None),
            P(AXES, None),
            P(AXES),
            P(AXES),
            P(),
        ),
        out_specs=(P(AXES, None), P(AXES, None, None), P()),
        check_vma=False,
    )
```

time: 212 us -> 95.2 us (0.45)
  the two profiles are of different devices: /device:TPU:1 before, /device:TPU:29 now
where the time goes in v1:
time: 95.2 us; the launch traced here: 94.9 us
  Pallas kernels  84.1 us (88%)
  local copies, waits for them, and re-layouts  6.25 us (7%)
  other arithmetic  3.83 us (4%)
    pallas_call x1, Pallas kernels, on_device(): pl.pallas_call(functools.partial(join_kernel, n, tiles, cap, group, q), o...  80.3 us
    unnamed x3, local copies, waits for them, and re-layouts  4.63 us
    pallas_call x1, Pallas kernels, on_device(): pl.pallas_call(functools.partial(pack_kernel, n, cap), out_shape=jax.Shap...  3.73 us

profile of v1, /device:TPU:29, one launch (start us, length us, event | category | flops | bytes accessed | tf_op | source)
XLA Modules:
  0.0 94.9 jit_solution(14314633977711502920)
XLA Ops:
  0.6 0.1 pad.17.clone
  0.7 1.0 %select_reduce_fusion = s32[192]{0:T(256)S(1)} fusion(s32[2048]{0:T(1024)} %param.15, s32[192]{0:T(256)} %param.14), kind=kLoop, calls=%fused_computation | loop fusion | flops 1179456 | bytes 9728 | tf_op jit(solution)/shard_map/reduce_sum | solution.py:174
  1.8 1.1 %convert_reduce_fusion = s32[192]{0:T(256)S(1)} fusion(s32[192,256]{1,0:T(8,128)} %valid_ref.1, s32[192]{0:T(256)} %param.13), kind=kLoop, calls=%fused_computation.4 | loop fusion | flops 245568 | bytes 198144 | tf_op jit(solution)/shard_map/reduce_sum | solution.py:170
  2.9 0.2 convert_reduce_fusion.1
  3.1 0.6 multiply_add_fusion.1.slot_ref
  3.7 0.2 select_reduce_fusion.1
  3.9 0.1 convert_element_type.30
  4.0 0.7 fusion.3.meta_ref
  4.7 1.4 %copy.13.live_count_ref = s32[192,1]{1,0:T(8,128)} copy(s32[192,1]{0,1:T(1,128)} %bitcast.15) | data formatting | bytes 1536 | tf_op jit(solution)/shard_map/broadcast_in_dim | solution.py:213
  6.2 3.7 %shard_map.103.send_ref = bf16[32,144,256]{2,1,0:T(8,128)(2,1)} custom-call(s32[1,192]{1,0:T(1,128)} %multiply_add_fusion.1.slot_ref, s32[192,1]{1,0:T(8,128)} %copy.13.live_count_ref, f32[192,256]{1,0:T(8,128)} %sdf_ref.1, f32[192,256]{1,0:T(8,128)} %weight_ref.1, f32[3,192,256]{2,1,0:T(8,128)} %color_ref.1, s32[192,256]{1,0:T(8,128)} %voxel_ref.1, ...), custom_call_target="tpu_custom_call" | custom-call | tf_op jit(solution)/shard_map/pallas_call | solution.py:208
  9.9 80.3 %shard_map.104 = (f32[64,512]{1,0:T(8,128)}, f32[3,64,512]{2,1,0:T(8,128)}, s32[16,128]{1,0:T(8,128)}) custom-call(bf16[32,144,256]{2,1,0:T(8,128)(2,1)} %shard_map.103.send_ref, f32[32,8,128]{2,1,0:T(8,128)} %fusion.3.meta_ref), custom_call_target="tpu_custom_call" | custom-call | tf_op jit(solution)/shard_map/pallas_call | solution.py:216
  90.2 1.6 %copy.18 = f32[64,512]{1,0:T(8,128)} copy(f32[64,512]{1,0:T(8,128)} %get-tuple-element.15) | data formatting | bytes 262144
  91.8 1.8 %copy.19 = f32[64,3,512]{2,0,1:T(8,128)} copy(f32[64,3,512]{2,0,1:T(8,128)} %bitcast.10) | data formatting | bytes 786432
  93.6 1.3 %copy.20 = s32[2048]{0:T(1024)} copy(s32[2048]{0:T(1024)} %bitcast.14) | data formatting | bytes 16384
  (9 shorter events, 0.1 us)

commit v2 on v1

v2 whole, which is shorter than its diff:
```python
import functools

import jax
import jax.numpy as jnp
from jax import lax
from jax.experimental import pallas as pl
from jax.experimental.pallas import tpu as pltpu
from jax.sharding import PartitionSpec as P

VOX = 512
HI = 8
LO = VOX // HI
CH = 5
AXES = ("view", "tile")
NT = (((1,), (1,)), ((), ()))


def pack_kernel(n, cap, slot_ref, live_count_ref, sdf_ref, weight_ref, color_ref, voxel_ref, valid_ref, out_ref):
    lists, points = sdf_ref.shape
    position = lax.broadcasted_iota(jnp.int32, (lists, points), 1)
    live = (position < live_count_ref[...]) & (valid_ref[...] == 1)
    scaled = jnp.where(live, weight_ref[...], 0.0)
    slots = lax.broadcasted_iota(jnp.int32, (n * cap, lists), 0)
    placement = jnp.where(slots == slot_ref[...], 1.0, 0.0).astype(jnp.bfloat16)
    for c in range(CH + 1):
        if c == 0:
            value = scaled
        elif c == 1:
            value = scaled * sdf_ref[...]
        elif c < CH:
            value = scaled * color_ref[c - 2]
        else:
            value = (voxel_ref[...] - VOX // 2).astype(jnp.float32)
        placed = jnp.dot(
            placement, value.astype(jnp.bfloat16), preferred_element_type=jnp.float32
        ).astype(jnp.bfloat16)
        for d in range(n):
            out_ref[d, c * cap : (c + 1) * cap, :] = placed[d * cap : (d + 1) * cap, :]


def join_kernel(
    views, tiles, cap, q, send_ref, meta_ref, tsdf_ref, color_ref, counts_ref,
    got, got_meta, block, parts, acc, dense_send, dense_got, hist, hist_got,
    send_sem, recv_sem, meta_send_sem, meta_recv_sem,
    dense_send_sem, dense_recv_sem, hist_send_sem, hist_recv_sem,
):
    view = lax.axis_index("view")
    tile = lax.axis_index("tile")
    points = send_ref.shape[-1]
    blocks_dev = tsdf_ref.shape[0]
    rows = CH * HI
    slots = tiles * cap
    half = HI // 2

    def view_of(k):
        step = views - 1 - k
        if views & (views - 1):
            return lax.rem(view + step, views)
        partner = 0
        bit = 1
        while bit < views:
            mine = (view // bit) % 2
            flip = (step // bit) % 2
            partner = partner + bit * (mine + flip - 2 * mine * flip)
            bit *= 2
        return partner

    def tile_of(i):
        return lax.rem(tile + i, tiles)

    barrier = pltpu.get_barrier_semaphore()

    @pl.loop(1, tiles)
    def _(i):
        pl.semaphore_signal(
            barrier, inc=1, device_id=(view, tile_of(i)), device_id_type=pl.DeviceIdType.MESH
        )

    @pl.loop(0, views - 1)
    def _(k):
        pl.semaphore_signal(
            barrier, inc=1, device_id=(view_of(k), tile), device_id_type=pl.DeviceIdType.MESH
        )

    def own_copy(k):
        return pltpu.make_async_copy(
            send_ref.at[view_of(k) * tiles + tile], got.at[k * tiles], recv_sem.at[k * tiles]
        )

    own_meta = pltpu.make_async_copy(meta_ref.at[tile], got_meta.at[0], meta_recv_sem.at[0])
    own_meta.start()

    @pl.loop(0, views)
    def _(k):
        own_copy(k).start()

    hist[...] = jnp.zeros_like(hist)
    pl.semaphore_wait(barrier, tiles - 1 + views - 1)

    def meta_copy(i):
        return pltpu.make_async_remote_copy(
            src_ref=meta_ref.at[tile_of(i)], dst_ref=got_meta.at[i],
            send_sem=meta_send_sem.at[i], recv_sem=meta_recv_sem.at[i],
            device_id=(view, tile_of(i)), device_id_type=pl.DeviceIdType.MESH,
        )

    def points_copy(k, i):
        at = k * tiles + i
        return pltpu.make_async_remote_copy(
            src_ref=send_ref.at[view_of(k) * tiles + tile_of(i)], dst_ref=got.at[at],
            send_sem=send_sem.at[at], recv_sem=recv_sem.at[at],
            device_id=(view, tile_of(i)), device_id_type=pl.DeviceIdType.MESH,
        )

    def dense_copy(k):
        return pltpu.make_async_remote_copy(
            src_ref=dense_send.at[k], dst_ref=dense_got.at[k],
            send_sem=dense_send_sem.at[k], recv_sem=dense_recv_sem.at[k],
            device_id=(view_of(k), tile), device_id_type=pl.DeviceIdType.MESH,
        )

    def hist_copy(k):
        return pltpu.make_async_remote_copy(
            src_ref=hist, dst_ref=hist_got.at[k],
            send_sem=hist_send_sem.at[k], recv_sem=hist_recv_sem.at[k],
            device_id=(view_of(k), tile), device_id_type=pl.DeviceIdType.MESH,
        )

    @pl.loop(1, tiles)
    def _(i):
        meta_copy(i).start()

    @pl.loop(0, views)
    def _(k):
        @pl.loop(1, tiles)
        def _(i):
            points_copy(k, i).start()

    hi_rows = lax.broadcasted_iota(jnp.int32, (HI, points), 0)
    hi_ids = jnp.where(hi_rows < half, 2 * hi_rows, 2 * hi_rows - (HI - 1)).astype(jnp.float32)
    lo_ids = lax.broadcasted_iota(jnp.int32, (LO, points), 0).astype(jnp.float32)
    lanes = q * 128
    hist_hi = lax.broadcasted_iota(jnp.int32, (hist.shape[0], lanes), 0).astype(jnp.float32)
    hist_lo = lax.broadcasted_iota(jnp.int32, (128, lanes), 0).astype(jnp.float32)
    row_ids = lax.broadcasted_iota(jnp.int32, (blocks_dev, slots), 0).astype(jnp.float32)

    @pl.loop(0, tiles)
    def _(j):
        pltpu.make_async_copy(got_meta.at[j], got_meta.at[j], meta_recv_sem.at[j]).wait()
        meta = got_meta[j]
        storage = jnp.concatenate([meta[views + k : views + k + 1, :] for k in range(q)], axis=1)
        counts = jnp.concatenate(
            [meta[views + q + k : views + q + k + 1, :] for k in range(q)], axis=1
        )
        s_hi = jnp.floor(storage * (1.0 / 128))
        s_lo = storage - s_hi * 128.0
        a = jnp.where(s_hi == hist_hi, counts, 0.0).astype(jnp.bfloat16)
        b = jnp.where(s_lo == hist_lo, 1.0, 0.0).astype(jnp.bfloat16)
        hist[...] += lax.dot_general(a, b, NT, preferred_element_type=jnp.float32)

    def one_source(k, j):
        at = k * tiles + j
        pltpu.make_async_copy(got.at[at], got.at[at], recv_sem.at[at]).wait()
        block[...] = got[at].astype(jnp.float32)
        voxel = block[CH * cap : (CH + 1) * cap, :] + float(VOX // 2)
        high = jnp.floor(voxel * (1.0 / LO))
        low = voxel - high * float(LO)
        for s in range(cap):
            mask = jnp.broadcast_to(high[s : s + 1, :], (HI, points)) == hi_ids
            a = jnp.concatenate(
                [
                    jnp.where(
                        mask,
                        jnp.broadcast_to(block[c * cap + s : c * cap + s + 1, :], (HI, points)),
                        0.0,
                    )
                    for c in range(CH)
                ],
                axis=0,
            ).astype(jnp.bfloat16)
            b = jnp.where(
                jnp.broadcast_to(low[s : s + 1, :], (LO, points)) == lo_ids, 1.0, 0.0
            ).astype(jnp.bfloat16)
            parts[pl.ds(j * cap + s, rows, stride=slots), :] = lax.dot_general(
                a, b, NT, preferred_element_type=jnp.float32
            )

    @pl.loop(0, views)
    def _(k):
        @pl.loop(0, tiles)
        def _(j):
            one_source(k, j)

        @pl.when(k == 0)
        def _():
            @pl.loop(0, views - 1)
            def _(v):
                hist_copy(v).start()

        row = jnp.concatenate(
            [got_meta[j, pl.ds(k, 1), 0:cap] for j in range(tiles)], axis=1
        )
        hot = jnp.where(row == row_ids, 1.0, 0.0).astype(jnp.bfloat16)
        for c in range(CH):
            for h in range(half):
                pair = [
                    jnp.dot(
                        hot,
                        parts[r * slots : (r + 1) * slots, :].astype(jnp.bfloat16),
                        preferred_element_type=jnp.float32,
                    )
                    for r in (c * HI + h, c * HI + half + h)
                ]
                acc[c * half + h] = jnp.concatenate(pair, axis=1)

        @pl.when(k < views - 1)
        def _():
            dense_send[k] = acc[...].astype(jnp.bfloat16)
            dense_copy(k).start()

    @pl.loop(0, views - 1)
    def _(k):
        dense_copy(k).wait_recv()
        acc[...] += dense_got[k].astype(jnp.float32)

    for h in range(half):
        at = slice(h * 2 * LO, (h + 1) * 2 * LO)
        divisor = jnp.maximum(acc[h], 1.0)
        tsdf_ref[:, at] = acc[half + h] / divisor
        for c in range(3):
            color_ref[c, :, at] = acc[(2 + c) * half + h] / divisor

    total = hist[...]
    for k in range(views - 1):
        hist_copy(k).wait_recv()
        total += hist_got[k]
    counts_ref[...] = total.astype(jnp.int32)

    @pl.loop(1, tiles)
    def _(i):
        meta_copy(i).wait_send()

    @pl.loop(0, views)
    def _(k):
        @pl.loop(1, tiles)
        def _(i):
            points_copy(k, i).wait_send()

    @pl.loop(0, views - 1)
    def _(k):
        dense_copy(k).wait_send()
        hist_copy(k).wait_send()


def on_device(tiles, sdf_value, weight, color, voxel_index, valid, list_count, list_key, owner_slot):
    lists, points = sdf_value.shape
    n = lax.axis_size(AXES)
    blocks_all = owner_slot.shape[0]
    blocks_dev = blocks_all // n
    cap = 4 * lists // n
    q = -(-lists // 128)
    views = n // tiles

    position = jnp.arange(points, dtype=jnp.int32)
    live_points = jnp.sum(
        ((position[None, :] < list_count[:, None]) & (valid == 1)).astype(jnp.int32), axis=1
    )
    key_match = list_key[:, None] == jnp.arange(blocks_all, dtype=jnp.int32)[None, :]
    storage = jnp.sum(jnp.where(key_match, owner_slot[None, :], 0), axis=1)
    owner = storage // blocks_dev
    row = storage % blocks_dev
    ids = jnp.arange(lists, dtype=jnp.int32)
    arrival = jnp.sum(
        ((owner[:, None] == owner[None, :]) & (ids[None, :] < ids[:, None])).astype(jnp.int32), axis=1
    )
    slot = owner * cap + arrival
    slot_row = (
        jnp.max(
            jnp.where(
                slot[None, :] == jnp.arange(n * cap, dtype=jnp.int32)[:, None], row[None, :], -1
            ),
            axis=1,
        )
        .astype(jnp.float32)
        .reshape(n, 1, cap)
    )
    slot_row = jnp.pad(slot_row, ((0, 0), (0, 0), (0, 128 - cap)), constant_values=-1.0)

    def lane_rows(x):
        x = jnp.pad(x.astype(jnp.float32), (0, q * 128 - lists)).reshape(1, q, 128)
        return jnp.broadcast_to(x, (tiles, q, 128))

    steps = jnp.arange(views - 1, -1, -1, dtype=jnp.int32)
    my_view = lax.axis_index("view")
    if views & (views - 1):
        order = (my_view + steps) % views
    else:
        order = my_view ^ steps
    by_view = jnp.take(slot_row.reshape(views, tiles, 128), order, axis=0)
    by_tile = jnp.swapaxes(by_view, 0, 1)
    meta_rows = -(-(views + 2 * q) // 8) * 8
    meta = jnp.concatenate(
        [
            by_tile,
            lane_rows(storage),
            lane_rows(live_points),
            jnp.zeros((tiles, meta_rows - views - 2 * q, 128), jnp.float32),
        ],
        axis=1,
    )
    send = pl.pallas_call(
        functools.partial(pack_kernel, n, cap),
        out_shape=jax.ShapeDtypeStruct((n, (CH + 1) * cap, points), jnp.bfloat16),
        in_specs=[pl.BlockSpec(memory_space=pltpu.VMEM)] * 7,
        out_specs=pl.BlockSpec(memory_space=pltpu.VMEM),
    )(slot[None, :], list_count[:, None], sdf_value, weight, color, voxel_index, valid)

    rows = CH * HI
    tsdf, joined, counts = pl.pallas_call(
        functools.partial(join_kernel, views, tiles, cap, q),
        out_shape=(
            jax.ShapeDtypeStruct((blocks_dev, VOX), jnp.float32),
            jax.ShapeDtypeStruct((3, blocks_dev, VOX), jnp.float32),
            jax.ShapeDtypeStruct((blocks_all // 128, 128), jnp.int32),
        ),
        in_specs=[pl.BlockSpec(memory_space=pl.ANY)] * 2,
        out_specs=(pl.BlockSpec(memory_space=pltpu.VMEM),) * 3,
        scratch_shapes=[
            pltpu.VMEM((n, (CH + 1) * cap, points), jnp.bfloat16),
            pltpu.VMEM((tiles, meta_rows, 128), jnp.float32),
            pltpu.VMEM(((CH + 1) * cap, points), jnp.float32),
            pltpu.VMEM((rows * tiles * cap, LO), jnp.float32),
            pltpu.VMEM((rows // 2, blocks_dev, 2 * LO), jnp.float32),
            pltpu.VMEM((views - 1, rows // 2, blocks_dev, 2 * LO), jnp.bfloat16),
            pltpu.VMEM((views - 1, rows // 2, blocks_dev, 2 * LO), jnp.bfloat16),
            pltpu.VMEM((blocks_all // 128, 128), jnp.float32),
            pltpu.VMEM((views - 1, blocks_all // 128, 128), jnp.float32),
            pltpu.SemaphoreType.DMA((n,)),
            pltpu.SemaphoreType.DMA((n,)),
            pltpu.SemaphoreType.DMA((tiles,)),
            pltpu.SemaphoreType.DMA((tiles,)),
            pltpu.SemaphoreType.DMA((views - 1,)),
            pltpu.SemaphoreType.DMA((views - 1,)),
            pltpu.SemaphoreType.DMA((views - 1,)),
            pltpu.SemaphoreType.DMA((views - 1,)),
        ],
        compiler_params=pltpu.CompilerParams(collective_id=0, has_side_effects=True),
    )(send, meta)
    return tsdf, jnp.swapaxes(joined, 0, 1), counts.reshape(blocks_all)


def solution(mesh):
    return jax.shard_map(
        functools.partial(on_device, mesh.shape["tile"]),
        mesh=mesh,
        in_specs=(
            P(AXES, None),
            P(AXES, None),
            P(None, AXES, None),
            P(AXES, None),
            P(AXES, None),
            P(AXES),
            P(AXES),
            P(),
        ),
        out_specs=(P(AXES, None), P(AXES, None, None), P()),
        check_vma=False,
    )
```

time: 95.2 us -> 64.2 us (0.67)
  the two profiles are of different devices: /device:TPU:29 before, /device:TPU:1 now
where the time goes in v2:
time: 64.2 us; the launch traced here: 63.8 us
  Pallas kernels  52.5 us (82%)
  local copies, waits for them, and re-layouts  6.72 us (10%)
  other arithmetic  3.83 us (6%)
  between operations  0.75 us (1%)
    pallas_call x1, Pallas kernels, on_device(): pl.pallas_call(functools.partial(join_kernel, views, tiles, cap, q), out_...  48.8 us
    unnamed x3, local copies, waits for them, and re-layouts  4.63 us
    pallas_call x1, Pallas kernels, on_device(): pl.pallas_call(functools.partial(pack_kernel, n, cap), out_shape=jax.Shap...  3.73 us
    broadcast_in_dim x1, local copies, waits for them, and re-layouts, on_device(): list_count[:, None]  1.44 us

profile of v2, /device:TPU:1, one launch (start us, length us, event | category | flops | bytes accessed | tf_op | source)
XLA Modules:
  0.0 63.8 jit_solution(13874608640983056836)
XLA Ops:
  0.7 1.0 %select_reduce_fusion = s32[192]{0:T(256)S(1)} fusion(s32[2048]{0:T(1024)} %param.15, s32[192]{0:T(256)} %param.14), kind=kLoop, calls=%fused_computation.1 | loop fusion | flops 1179456 | bytes 9728 | tf_op jit(solution)/shard_map/reduce_sum | solution.py:269
  1.7 1.1 %convert_reduce_fusion = s32[192]{0:T(256)S(1)} fusion(s32[192,256]{1,0:T(8,128)} %valid_ref.1, s32[192]{0:T(256)} %param.13), kind=kLoop, calls=%fused_computation.5 | loop fusion | flops 245568 | bytes 198144 | tf_op jit(solution)/shard_map/reduce_sum | solution.py:265
  2.9 0.2 convert_reduce_fusion.1
  3.1 0.6 multiply_add_fusion.1.slot_ref
  3.6 0.2 select_reduce_fusion.1
  3.9 0.1 convert_element_type.25
  3.9 0.6 gather_fusion
  4.5 0.1 select_bitcast_fusion
  4.6 0.6 pad_maximum_fusion.meta_ref
  5.2 1.4 %copy.13.live_count_ref = s32[192,1]{1,0:T(8,128)} copy(s32[192,1]{0,1:T(1,128)} %bitcast.17) | data formatting | bytes 1536 | tf_op jit(solution)/shard_map/broadcast_in_dim | solution.py:316
  6.7 3.7 %shard_map.103.send_ref = bf16[32,144,256]{2,1,0:T(8,128)(2,1)} custom-call(s32[1,192]{1,0:T(1,128)} %multiply_add_fusion.1.slot_ref, s32[192,1]{1,0:T(8,128)} %copy.13.live_count_ref, f32[192,256]{1,0:T(8,128)} %sdf_ref.1, f32[192,256]{1,0:T(8,128)} %weight_ref.1, f32[3,192,256]{2,1,0:T(8,128)} %color_ref.1, s32[192,256]{1,0:T(8,128)} %voxel_ref.1, ...), custom_call_target="tpu_custom_call" | custom-call | tf_op jit(solution)/shard_map/pallas_call | solution.py:311
  10.4 48.8 %shard_map.104 = (f32[64,512]{1,0:T(8,128)}, f32[3,64,512]{2,1,0:T(8,128)}, s32[16,128]{1,0:T(8,128)}) custom-call(bf16[32,144,256]{2,1,0:T(8,128)(2,1)} %shard_map.103.send_ref, f32[8,8,128]{2,1,0:T(8,128)} %pad_maximum_fusion.meta_ref), custom_call_target="tpu_custom_call" | custom-call | tf_op jit(solution)/shard_map/pallas_call | solution.py:319
  59.2 1.6 %copy.18 = f32[64,512]{1,0:T(8,128)} copy(f32[64,512]{1,0:T(8,128)} %get-tuple-element.15) | data formatting | bytes 262144
  60.7 1.8 %copy.19 = f32[64,3,512]{2,0,1:T(8,128)} copy(f32[64,3,512]{2,0,1:T(8,128)} %bitcast.13) | data formatting | bytes 786432
  62.5 1.3 %copy.20 = s32[2048]{0:T(1024)} copy(s32[2048]{0:T(1024)} %bitcast.16) | data formatting | bytes 16384
  (12 shorter events, 0.1 us)

commit v3 on v2

--- a/solution.py
+++ b/solution.py
@@ -13,43 +13,36 @@
 CH = 5
 AXES = ("view", "tile")
 NT = (((1,), (1,)), ((), ()))
-
-
-def pack_kernel(n, cap, slot_ref, live_count_ref, sdf_ref, weight_ref, color_ref, voxel_ref, valid_ref, out_ref):
-    lists, points = sdf_ref.shape
-    position = lax.broadcasted_iota(jnp.int32, (lists, points), 1)
-    live = (position < live_count_ref[...]) & (valid_ref[...] == 1)
-    scaled = jnp.where(live, weight_ref[...], 0.0)
-    slots = lax.broadcasted_iota(jnp.int32, (n * cap, lists), 0)
-    placement = jnp.where(slots == slot_ref[...], 1.0, 0.0).astype(jnp.bfloat16)
-    for c in range(CH + 1):
-        if c == 0:
-            value = scaled
-        elif c == 1:
-            value = scaled * sdf_ref[...]
-        elif c < CH:
-            value = scaled * color_ref[c - 2]
-        else:
-            value = (voxel_ref[...] - VOX // 2).astype(jnp.float32)
-        placed = jnp.dot(
-            placement, value.astype(jnp.bfloat16), preferred_element_type=jnp.float32
-        ).astype(jnp.bfloat16)
-        for d in range(n):
-            out_ref[d, c * cap : (c + 1) * cap, :] = placed[d * cap : (d + 1) * cap, :]
+TN = (((0,), (0,)), ((), ()))
+NN = (((1,), (0,)), ((), ()))
+
+
+def finish_kernel(sums_ref, hist_ref, tsdf_ref, color_ref, counts_ref):
+    half = HI // 2
+    for h in range(half):
+        at = slice(h * 2 * LO, (h + 1) * 2 * LO)
+        divisor = jnp.maximum(sums_ref[h], 1.0)
+        tsdf_ref[:, at] = sums_ref[half + h] / divisor
+        for c in range(3):
+            color_ref[c, :, at] = sums_ref[(2 + c) * half + h] / divisor
+    counts_ref[...] = hist_ref[...].astype(jnp.int32)
 
 
 def join_kernel(
-    views, tiles, cap, q, send_ref, meta_ref, tsdf_ref, color_ref, counts_ref,
-    got, got_meta, block, parts, acc, dense_send, dense_got, hist, hist_got,
+    views, tiles, cap, q, key_ref, owner_ref, count_ref, sdf_ref, weight_ref, color_ref,
+    voxel_ref, valid_ref, acc, total_ref,
+    send_ref, meta_ref, values, got, got_meta, block, parts, dense_send, dense_got, hist, hist_got,
     send_sem, recv_sem, meta_send_sem, meta_recv_sem,
     dense_send_sem, dense_recv_sem, hist_send_sem, hist_recv_sem,
 ):
     view = lax.axis_index("view")
     tile = lax.axis_index("tile")
     points = send_ref.shape[-1]
-    blocks_dev = tsdf_ref.shape[0]
+    lists = sdf_ref.shape[0]
+    blocks_dev = acc.shape[1]
     rows = CH * HI
     slots = tiles * cap
+    pitch = slots + 8
     half = HI // 2
 
     def view_of(k):
@@ -84,8 +77,70 @@
 
     def own_copy(k):
         return pltpu.make_async_copy(
-            send_ref.at[view_of(k) * tiles + tile], got.at[k * tiles], recv_sem.at[k * tiles]
-        )
+            send_ref.at[k * tiles + tile], got.at[k * tiles], recv_sem.at[k * tiles]
+        )
+
+    bf16, f32 = jnp.bfloat16, jnp.float32
+
+    def iota(shape, dim):
+        return lax.broadcasted_iota(jnp.int32, shape, dim).astype(f32)
+
+    def dot(a, b, dims):
+        return lax.dot_general(a, b, dims, preferred_element_type=f32)
+
+    key = key_ref[...].astype(f32)
+    key_hi = jnp.floor(key * (1.0 / 128))
+    key_lo = key - key_hi * 128.0
+    table = owner_ref[...].astype(f32)
+    table_hi = jnp.floor(table * (1.0 / 64))
+    table_lo = table - table_hi * 64.0
+    hot_hi = jnp.where(key_hi == iota((table.shape[0], lists), 0), 1.0, 0.0).astype(bf16)
+    found = 64.0 * dot(table_hi.astype(bf16), hot_hi, TN) + dot(table_lo.astype(bf16), hot_hi, TN)
+    storage = jnp.sum(
+        jnp.where(key_lo == iota((128, lists), 0), found, 0.0), axis=0, keepdims=True
+    )
+    owner = jnp.floor((storage + 0.5) * (1.0 / blocks_dev))
+    block_row = storage - owner * blocks_dev
+    is_owner = owner == iota((views * tiles, lists), 0)
+    before = jnp.where(iota((lists, lists), 0) < iota((lists, lists), 1), 1.0, 0.0).astype(bf16)
+    earlier = dot(jnp.where(is_owner, 1.0, 0.0).astype(bf16), before, NN)
+    arrival = jnp.sum(jnp.where(is_owner, earlier, 0.0), axis=0, keepdims=True)
+    slot = owner * cap + arrival
+
+    diagonal = iota((lists, lists), 0) == iota((lists, lists), 1)
+    list_count = dot(
+        jnp.where(diagonal, count_ref[...].astype(f32), 0.0).astype(bf16),
+        jnp.ones((lists, points), bf16), NN,
+    )
+    live = (iota((lists, points), 1) < list_count) & (valid_ref[...] == 1)
+    scaled = jnp.where(live, weight_ref[...], 0.0)
+    values[0] = scaled.astype(bf16)
+    values[1] = (scaled * sdf_ref[...]).astype(bf16)
+    for c in range(3):
+        values[2 + c] = (scaled * color_ref[c]).astype(bf16)
+    values[CH] = (voxel_ref[...] - VOX // 2).astype(f32).astype(bf16)
+    live_count = dot(jnp.ones((8, points), bf16), jnp.where(live, 1.0, 0.0).astype(bf16), NT)[0:1]
+
+    meta_ref[...] = jnp.zeros_like(meta_ref)
+    for j in range(q):
+        at = slice(j * 128, min(lists, (j + 1) * 128))
+        for t in range(tiles):
+            meta_ref[t, views + j : views + j + 1, 0 : at.stop - at.start] = storage[:, at]
+            meta_ref[t, views + q + j : views + q + j + 1, 0 : at.stop - at.start] = live_count[:, at]
+    row_code = jnp.broadcast_to(block_row + 1.0, (8, lists)).astype(bf16)
+
+    for k in range(views):
+        first = (view_of(k) * slots).astype(f32)
+        placement = jnp.where(iota((slots, lists), 0) + first == slot, 1.0, 0.0).astype(bf16)
+        slot_rows = dot(row_code, placement, NT) - 1.0
+        for t in range(tiles):
+            meta_ref[t, k : k + 1, 0:cap] = slot_rows[0:1, t * cap : (t + 1) * cap]
+        for c in range(CH + 1):
+            placed = dot(placement, values[c], NN).astype(bf16)
+            for t in range(tiles):
+                send_ref[k * tiles + t, c * cap : (c + 1) * cap, :] = placed[t * cap : (t + 1) * cap]
+    hist[...] = jnp.zeros_like(hist)
+    pl.semaphore_wait(barrier, tiles - 1 + views - 1)
 
     own_meta = pltpu.make_async_copy(meta_ref.at[tile], got_meta.at[0], meta_recv_sem.at[0])
     own_meta.start()
@@ -93,9 +148,6 @@
     @pl.loop(0, views)
     def _(k):
         own_copy(k).start()
-
-    hist[...] = jnp.zeros_like(hist)
-    pl.semaphore_wait(barrier, tiles - 1 + views - 1)
 
     def meta_copy(i):
         return pltpu.make_async_remote_copy(
@@ -107,7 +159,7 @@
     def points_copy(k, i):
         at = k * tiles + i
         return pltpu.make_async_remote_copy(
-            src_ref=send_ref.at[view_of(k) * tiles + tile_of(i)], dst_ref=got.at[at],
+            src_ref=send_ref.at[k * tiles + tile_of(i)], dst_ref=got.at[at],
             send_sem=send_sem.at[at], recv_sem=recv_sem.at[at],
             device_id=(view, tile_of(i)), device_id_type=pl.DeviceIdType.MESH,
         )
@@ -181,7 +233,7 @@
             b = jnp.where(
                 jnp.broadcast_to(low[s : s + 1, :], (LO, points)) == lo_ids, 1.0, 0.0
             ).astype(jnp.bfloat16)
-            parts[pl.ds(j * cap + s, rows, stride=slots), :] = lax.dot_general(
+            parts[pl.ds(j * cap + s, rows, stride=pitch), :] = lax.dot_general(
                 a, b, NT, preferred_element_type=jnp.float32
             )
 
@@ -206,7 +258,7 @@
                 pair = [
                     jnp.dot(
                         hot,
-                        parts[r * slots : (r + 1) * slots, :].astype(jnp.bfloat16),
+                        parts[r * pitch : r * pitch + slots, :].astype(jnp.bfloat16),
                         preferred_element_type=jnp.float32,
                     )
                     for r in (c * HI + h, c * HI + half + h)
@@ -223,18 +275,11 @@
         dense_copy(k).wait_recv()
         acc[...] += dense_got[k].astype(jnp.float32)
 
-    for h in range(half):
-        at = slice(h * 2 * LO, (h + 1) * 2 * LO)
-        divisor = jnp.maximum(acc[h], 1.0)
-        tsdf_ref[:, at] = acc[half + h] / divisor
-        for c in range(3):
-            color_ref[c, :, at] = acc[(2 + c) * half + h] / divisor
-
     total = hist[...]
     for k in range(views - 1):
         hist_copy(k).wait_recv()
         total += hist_got[k]
-    counts_ref[...] = total.astype(jnp.int32)
+    total_ref[...] = total
 
     @pl.loop(1, tiles)
     def _(i):
@@ -261,76 +306,27 @@
     q = -(-lists // 128)
     views = n // tiles
 
-    position = jnp.arange(points, dtype=jnp.int32)
-    live_points = jnp.sum(
-        ((position[None, :] < list_count[:, None]) & (valid == 1)).astype(jnp.int32), axis=1
-    )
-    key_match = list_key[:, None] == jnp.arange(blocks_all, dtype=jnp.int32)[None, :]
-    storage = jnp.sum(jnp.where(key_match, owner_slot[None, :], 0), axis=1)
-    owner = storage // blocks_dev
-    row = storage % blocks_dev
-    ids = jnp.arange(lists, dtype=jnp.int32)
-    arrival = jnp.sum(
-        ((owner[:, None] == owner[None, :]) & (ids[None, :] < ids[:, None])).astype(jnp.int32), axis=1
-    )
-    slot = owner * cap + arrival
-    slot_row = (
-        jnp.max(
-            jnp.where(
-                slot[None, :] == jnp.arange(n * cap, dtype=jnp.int32)[:, None], row[None, :], -1
-            ),
-            axis=1,
-        )
-        .astype(jnp.float32)
-        .reshape(n, 1, cap)
-    )
-    slot_row = jnp.pad(slot_row, ((0, 0), (0, 0), (0, 128 - cap)), constant_values=-1.0)
-
-    def lane_rows(x):
-        x = jnp.pad(x.astype(jnp.float32), (0, q * 128 - lists)).reshape(1, q, 128)
-        return jnp.broadcast_to(x, (tiles, q, 128))
-
-    steps = jnp.arange(views - 1, -1, -1, dtype=jnp.int32)
-    my_view = lax.axis_index("view")
-    if views & (views - 1):
-        order = (my_view + steps) % views
-    else:
-        order = my_view ^ steps
-    by_view = jnp.take(slot_row.reshape(views, tiles, 128), order, axis=0)
-    by_tile = jnp.swapaxes(by_view, 0, 1)
     meta_rows = -(-(views + 2 * q) // 8) * 8
-    meta = jnp.concatenate(
-        [
-            by_tile,
-            lane_rows(storage),
-            lane_rows(live_points),
-            jnp.zeros((tiles, meta_rows - views - 2 * q, 128), jnp.float32),
-        ],
-        axis=1,
-    )
-    send = pl.pallas_call(
-        functools.partial(pack_kernel, n, cap),
-        out_shape=jax.ShapeDtypeStruct((n, (CH + 1) * cap, points), jnp.bfloat16),
-        in_specs=[pl.BlockSpec(memory_space=pltpu.VMEM)] * 7,
-        out_specs=pl.BlockSpec(memory_space=pltpu.VMEM),
-    )(slot[None, :], list_count[:, None], sdf_value, weight, color, voxel_index, valid)
-
+    payload = (n, (CH + 1) * cap, points)
+    wide = (blocks_all // 128, 128)
     rows = CH * HI
-    tsdf, joined, counts = pl.pallas_call(
+    vmem = pl.BlockSpec(memory_space=pltpu.VMEM)
+    sums, total = pl.pallas_call(
         functools.partial(join_kernel, views, tiles, cap, q),
         out_shape=(
-            jax.ShapeDtypeStruct((blocks_dev, VOX), jnp.float32),
-            jax.ShapeDtypeStruct((3, blocks_dev, VOX), jnp.float32),
-            jax.ShapeDtypeStruct((blocks_all // 128, 128), jnp.int32),
+            jax.ShapeDtypeStruct((rows // 2, blocks_dev, 2 * LO), jnp.float32),
+            jax.ShapeDtypeStruct(wide, jnp.float32),
         ),
-        in_specs=[pl.BlockSpec(memory_space=pl.ANY)] * 2,
-        out_specs=(pl.BlockSpec(memory_space=pltpu.VMEM),) * 3,
+        in_specs=[vmem] * 8,
+        out_specs=(vmem,) * 2,
         scratch_shapes=[
-            pltpu.VMEM((n, (CH + 1) * cap, points), jnp.bfloat16),
+            pltpu.VMEM(payload, jnp.bfloat16),
+            pltpu.VMEM((tiles, meta_rows, 128), jnp.float32),
+            pltpu.VMEM((CH + 1, lists, points), jnp.bfloat16),
+            pltpu.VMEM(payload, jnp.bfloat16),
             pltpu.VMEM((tiles, meta_rows, 128), jnp.float32),
             pltpu.VMEM(((CH + 1) * cap, points), jnp.float32),
-            pltpu.VMEM((rows * tiles * cap, LO), jnp.float32),
-            pltpu.VMEM((rows // 2, blocks_dev, 2 * LO), jnp.float32),
+            pltpu.VMEM((rows * (tiles * cap + 8), LO), jnp.float32),
             pltpu.VMEM((views - 1, rows // 2, blocks_dev, 2 * LO), jnp.bfloat16),
             pltpu.VMEM((views - 1, rows // 2, blocks_dev, 2 * LO), jnp.bfloat16),
             pltpu.VMEM((blocks_all // 128, 128), jnp.float32),
@@ -345,7 +341,20 @@
             pltpu.SemaphoreType.DMA((views - 1,)),
         ],
         compiler_params=pltpu.CompilerParams(collective_id=0, has_side_effects=True),
-    )(send, meta)
+    )(
+        list_key.reshape(1, lists), owner_slot.reshape(wide), list_count.reshape(1, lists),
+        sdf_value, weight, color, voxel_index, valid,
+    )
+    tsdf, joined, counts = pl.pallas_call(
+        finish_kernel,
+        out_shape=(
+            jax.ShapeDtypeStruct((blocks_dev, VOX), jnp.float32),
+            jax.ShapeDtypeStruct((3, blocks_dev, VOX), jnp.float32),
+            jax.ShapeDtypeStruct(wide, jnp.int32),
+        ),
+        in_specs=[vmem] * 2,
+        out_specs=(vmem,) * 3,
+    )(sums, total)
     return tsdf, jnp.swapaxes(joined, 0, 1), counts.reshape(blocks_all)
 
 

time: 64.2 us -> 52.2 us (0.81)
  local copies, waits for them, and re-layouts: 6.72 us -> 0 us
  other arithmetic: 3.83 us -> 0 us
  Pallas kernels: 52.5 us -> 51.4 us
    unnamed x3 -> x0, local copies, waits for them, and re-layouts: 4.63 us -> none
    reduce_sum x3 -> x0, other arithmetic: 2.34 us -> none  [the longest x1 1.12 us: on_device(): jnp.sum(((position[None, :] < list_count[:, None]) & (valid == 1)).astype...]
    pallas_call x1, Pallas kernels: 3.73 us -> 1.94 us  [on_device(): pl.pallas_call(finish_kernel, out_shape=(jax.ShapeDtypeStruct((blocks_dev...]
    broadcast_in_dim x5 -> x0, local copies, waits for them, and re-layouts: 1.46 us -> none  [the longest x1 1.44 us: on_device(): list_count[:, None]]
    pallas_call x1, Pallas kernels: 48.8 us -> 49.5 us  [on_device(): pl.pallas_call(functools.partial(join_kernel, views, tiles, cap, q), out_...]
where the time goes in v3:
time: 52.2 us; the launch traced here: 52 us
  Pallas kernels  51.4 us (98%)
  between operations  0.64 us (1%)
    pallas_call x1, Pallas kernels, on_device(): pl.pallas_call(functools.partial(join_kernel, views, tiles, cap, q), out_...  49.5 us
    pallas_call x1, Pallas kernels, on_device(): pl.pallas_call(finish_kernel, out_shape=(jax.ShapeDtypeStruct((blocks_dev...  1.94 us

profile of v3, /device:TPU:1, one launch (start us, length us, event | category | flops | bytes accessed | tf_op | source)
XLA Modules:
  0.0 52.0 jit_solution(4383574558743857217)
XLA Ops:
  0.6 49.5 %shard_map.103 = (f32[20,64,128]{2,1,0:T(8,128)}, f32[16,128]{1,0:T(8,128)}) custom-call(s32[1,192]{1,0:T(1,128)} %bitcast.6, s32[16,128]{1,0:T(8,128)} %bitcast.5, s32[1,192]{1,0:T(1,128)} %bitcast.7, f32[192,256]{1,0:T(8,128)} %sdf_ref.1, f32[192,256]{1,0:T(8,128)} %weight_ref.1, f32[3,192,256]{2,1,0:T(8,128)} %color_ref.1, s32[192,256]{1,0:T(8,128)} %voxel_ref.1, ...), custom_call_target="tpu_custom_call" | custom-call | tf_op jit(solution)/shard_map/pallas_call | solution.py:314
  50.1 1.9 %shard_map.104 = (f32[64,512]{1,0:T(8,128)}, f32[3,64,512]{2,1,0:T(8,128)}, s32[16,128]{1,0:T(8,128)}) custom-call(f32[20,64,128]{2,1,0:T(8,128)} %get-tuple-element.8.sums_ref, f32[16,128]{1,0:T(8,128)} %get-tuple-element.9.hist_ref), custom_call_target="tpu_custom_call" | custom-call | tf_op jit(solution)/shard_map/pallas_call | solution.py:348

commit v4 on v3

--- a/solution.py
+++ b/solution.py
@@ -129,25 +129,14 @@
             meta_ref[t, views + q + j : views + q + j + 1, 0 : at.stop - at.start] = live_count[:, at]
     row_code = jnp.broadcast_to(block_row + 1.0, (8, lists)).astype(bf16)
 
+    def placement_of(k):
+        first = (view_of(k) * slots).astype(f32)
+        return jnp.where(iota((slots, lists), 0) + first == slot, 1.0, 0.0).astype(bf16)
+
     for k in range(views):
-        first = (view_of(k) * slots).astype(f32)
-        placement = jnp.where(iota((slots, lists), 0) + first == slot, 1.0, 0.0).astype(bf16)
-        slot_rows = dot(row_code, placement, NT) - 1.0
+        slot_rows = dot(row_code, placement_of(k), NT) - 1.0
         for t in range(tiles):
             meta_ref[t, k : k + 1, 0:cap] = slot_rows[0:1, t * cap : (t + 1) * cap]
-        for c in range(CH + 1):
-            placed = dot(placement, values[c], NN).astype(bf16)
-            for t in range(tiles):
-                send_ref[k * tiles + t, c * cap : (c + 1) * cap, :] = placed[t * cap : (t + 1) * cap]
-    hist[...] = jnp.zeros_like(hist)
-    pl.semaphore_wait(barrier, tiles - 1 + views - 1)
-
-    own_meta = pltpu.make_async_copy(meta_ref.at[tile], got_meta.at[0], meta_recv_sem.at[0])
-    own_meta.start()
-
-    @pl.loop(0, views)
-    def _(k):
-        own_copy(k).start()
 
     def meta_copy(i):
         return pltpu.make_async_remote_copy(
@@ -171,6 +160,17 @@
             device_id=(view_of(k), tile), device_id_type=pl.DeviceIdType.MESH,
         )
 
+    relaying = views == 4
+    outer = 1 - ((view + 1) // 2) % 2 if relaying else 0
+    relay_slot = views - 1
+
+    def relay_copy():
+        return pltpu.make_async_remote_copy(
+            src_ref=dense_send.at[0], dst_ref=dense_got.at[relay_slot],
+            send_sem=dense_send_sem.at[0], recv_sem=dense_recv_sem.at[relay_slot],
+            device_id=(view_of(views - 2), tile), device_id_type=pl.DeviceIdType.MESH,
+        )
+
     def hist_copy(k):
         return pltpu.make_async_remote_copy(
             src_ref=hist, dst_ref=hist_got.at[k],
@@ -178,15 +178,34 @@
             device_id=(view_of(k), tile), device_id_type=pl.DeviceIdType.MESH,
         )
 
-    @pl.loop(1, tiles)
-    def _(i):
-        meta_copy(i).start()
-
-    @pl.loop(0, views)
-    def _(k):
+    def send_parcels(k):
+        own_copy(k).start()
+
         @pl.loop(1, tiles)
         def _(i):
             points_copy(k, i).start()
+
+    hist[...] = jnp.zeros_like(hist)
+    for k in range(views):
+        placement = placement_of(k)
+        for c in range(CH + 1):
+            placed = dot(placement, values[c], NN).astype(bf16)
+            for t in range(tiles):
+                send_ref[k * tiles + t, c * cap : (c + 1) * cap, :] = placed[t * cap : (t + 1) * cap]
+        if k == 0:
+            pl.semaphore_wait(barrier, tiles - 1 + views - 1)
+            own_meta = pltpu.make_async_copy(
+                meta_ref.at[tile], got_meta.at[0], meta_recv_sem.at[0]
+            )
+            own_meta.start()
+
+            @pl.loop(1, tiles)
+            def _(i):
+                meta_copy(i).start()
+
+        else:
+            send_parcels(k - 1)
+    send_parcels(views - 1)
 
     hi_rows = lax.broadcasted_iota(jnp.int32, (HI, points), 0)
     hi_ids = jnp.where(hi_rows < half, 2 * hi_rows, 2 * hi_rows - (HI - 1)).astype(jnp.float32)
@@ -265,15 +284,41 @@
                 ]
                 acc[c * half + h] = jnp.concatenate(pair, axis=1)
 
+        if relaying:
+
+            @pl.when((k == 1) & (outer == 0))
+            def _():
+                relay_copy().wait_recv()
+                acc[...] += dense_got[relay_slot].astype(jnp.float32)
+
         @pl.when(k < views - 1)
         def _():
             dense_send[k] = acc[...].astype(jnp.bfloat16)
-            dense_copy(k).start()
-
-    @pl.loop(0, views - 1)
-    def _(k):
+            if relaying:
+
+                @pl.when((k == 0) & (outer == 1))
+                def _():
+                    relay_copy().start()
+
+                @pl.when((k > 0) | (outer == 0))
+                def _():
+                    dense_copy(k).start()
+
+            else:
+                dense_copy(k).start()
+
+    def add_arrived(k):
         dense_copy(k).wait_recv()
         acc[...] += dense_got[k].astype(jnp.float32)
+
+    if relaying:
+        pl.when(outer == 0)(functools.partial(add_arrived, 0))
+    else:
+        add_arrived(0)
+
+    @pl.loop(1, views - 1)
+    def _(k):
+        add_arrived(k)
 
     total = hist[...]
     for k in range(views - 1):
@@ -328,7 +373,7 @@
             pltpu.VMEM(((CH + 1) * cap, points), jnp.float32),
             pltpu.VMEM((rows * (tiles * cap + 8), LO), jnp.float32),
             pltpu.VMEM((views - 1, rows // 2, blocks_dev, 2 * LO), jnp.bfloat16),
-            pltpu.VMEM((views - 1, rows // 2, blocks_dev, 2 * LO), jnp.bfloat16),
+            pltpu.VMEM((views, rows // 2, blocks_dev, 2 * LO), jnp.bfloat16),
             pltpu.VMEM((blocks_all // 128, 128), jnp.float32),
             pltpu.VMEM((views - 1, blocks_all // 128, 128), jnp.float32),
             pltpu.SemaphoreType.DMA((n,)),
@@ -336,7 +381,7 @@
             pltpu.SemaphoreType.DMA((tiles,)),
             pltpu.SemaphoreType.DMA((tiles,)),
             pltpu.SemaphoreType.DMA((views - 1,)),
-            pltpu.SemaphoreType.DMA((views - 1,)),
+            pltpu.SemaphoreType.DMA((views,)),
             pltpu.SemaphoreType.DMA((views - 1,)),
             pltpu.SemaphoreType.DMA((views - 1,)),
         ],

time: 52.2 us -> 50.2 us (0.962)
  Pallas kernels: 51.4 us -> 49.4 us
    pallas_call x1, Pallas kernels: 49.5 us -> 47.5 us  [on_device(): pl.pallas_call(functools.partial(join_kernel, views, tiles, cap, q), out_...]
where the time goes in v4:
time: 50.2 us; the launch traced here: 50.1 us
  Pallas kernels  49.4 us (98%)
  between operations  0.64 us (1%)
    pallas_call x1, Pallas kernels, on_device(): pl.pallas_call(functools.partial(join_kernel, views, tiles, cap, q), out_...  47.5 us
    pallas_call x1, Pallas kernels, on_device(): pl.pallas_call(finish_kernel, out_shape=(jax.ShapeDtypeStruct((blocks_dev...  1.94 us

profile of v4, /device:TPU:1, one launch (start us, length us, event | category | flops | bytes accessed | tf_op | source)
XLA Modules:
  0.0 50.1 jit_solution(15134593474831472341)
XLA Ops:
  0.6 47.5 %shard_map.103 = (f32[20,64,128]{2,1,0:T(8,128)}, f32[16,128]{1,0:T(8,128)}) custom-call(s32[1,192]{1,0:T(1,128)} %bitcast.6, s32[16,128]{1,0:T(8,128)} %bitcast.5, s32[1,192]{1,0:T(1,128)} %bitcast.7, f32[192,256]{1,0:T(8,128)} %sdf_ref.1, f32[192,256]{1,0:T(8,128)} %weight_ref.1, f32[3,192,256]{2,1,0:T(8,128)} %color_ref.1, s32[192,256]{1,0:T(8,128)} %voxel_ref.1, ...), custom_call_target="tpu_custom_call" | custom-call | tf_op jit(solution)/shard_map/pallas_call | solution.py:359
  48.1 1.9 %shard_map.104 = (f32[64,512]{1,0:T(8,128)}, f32[3,64,512]{2,1,0:T(8,128)}, s32[16,128]{1,0:T(8,128)}) custom-call(f32[20,64,128]{2,1,0:T(8,128)} %get-tuple-element.8.sums_ref, f32[16,128]{1,0:T(8,128)} %get-tuple-element.9.hist_ref), custom_call_target="tpu_custom_call" | custom-call | tf_op jit(solution)/shard_map/pallas_call | solution.py:393
